TPU v7x, 256 devices: a whole 4x4x8 slice. The times are simulated.
256 devices in a mesh: chain: 64 (over z, x, core), term: 4 (over y).
Axes of the slice: x: 4, y: 4, z: 8, core: 2. Of those that a mesh axis runs over, the one named last changes fastest.
Arguments:
- psi_guess: float32 [64, 8, 128, 128], P('chain'), may hold values from -6 to 6
- transfer_raw: float32 [64, 8, 128, 128], P('chain'), may hold values from -6 to 6
- left_env: float32 [64, 32, 8, 128, 128], P('chain', 'term'), may hold values from -0.75 to 0.75
- right_env: float32 [64, 32, 8, 128, 128], P('chain', 'term'), may hold values from -0.75 to 0.75
- block_sizes: int32 [64, 2, 8], P('chain'), may hold values from 64 to 128
Outputs:
- psi_out: float32 [64, 8, 128, 128], P('chain', 'term')
- energy: float32 [64], P('chain')
All inputs are finite; a program needn't handle non-finite values.
Results may differ from a plain program's by a relative error of at most 0.0003.
Values sent between devices are 32-bit elements; how exact they have to be, the bound alone decides.
No kernel may reach another device: no remote copies, remote signals or barrier semaphores. Data moves between devices by JAX's collectives and lax.ppermute only.
A program may use at most 128 MiB of HBM per device.

v0:
```python
import math
import jax
import jax.numpy as jnp
from jax import lax
from jax.sharding import PartitionSpec as P

ITERS = 4
precise = lax.Precision.HIGHEST
twist_scale = 0.22
shrink = 1.047
epsilon = 1e-06


def from_behind(value, axis, steps):
    count = lax.axis_size(axis)
    leading, last = (max(0, -steps), min(count, count - steps))
    return lax.ppermute(value, axis, [(source, source + steps) for source in range(leading, last)])


def transfer(raw_normal):
    block_len = raw_normal.shape[-1]
    identity = jnp.eye(block_len, dtype=jnp.float32)
    skewed = (raw_normal - jnp.swapaxes(raw_normal, -1, -2)) * (
        twist_scale / math.sqrt(2.0 * block_len)
    )
    return (identity + skewed) / shrink


def symmetric(raw_normal):
    return 0.5 * (raw_normal + jnp.swapaxes(raw_normal, -1, -2))


def sector_mask(sizes_pair, block_len):
    positions = jnp.arange(block_len, dtype=jnp.int32)
    row_live = (positions[None, :] < sizes_pair[0][:, None]).astype(jnp.float32)
    col_live = (positions[None, :] < sizes_pair[1][:, None]).astype(jnp.float32)
    return row_live[:, :, None] * col_live[:, None, :]


def local(psi_guess, transfer_raw, left_env, right_env, block_sizes):
    blocks = transfer(transfer_raw[0])
    sectors = blocks.shape[0]
    block_len = blocks.shape[-1]
    identity = jnp.broadcast_to(jnp.eye(block_len, dtype=jnp.float32), blocks.shape)
    position = lax.axis_index("chain")
    segments = lax.axis_size("chain")
    from_left, left_blocks = from_behind((left_env[0], blocks), "chain", 1)
    from_right, right_blocks = from_behind((right_env[0], blocks), "chain", -1)
    is_first = position == 0
    is_last = position == segments - 1
    prefix = jnp.where(is_first, identity, left_blocks)
    suffix = jnp.where(is_last, identity, right_blocks)
    left_sym = symmetric(jnp.where(is_first, left_env[0], from_left))
    right_sym = symmetric(jnp.where(is_last, right_env[0], from_right))
    live_mask = sector_mask(block_sizes[0], block_len)
    groups = lax.axis_size("term")
    owned = sectors // groups
    offset = lax.axis_index("term") * owned
    volume = float(sectors * block_len * block_len)
    partway = jnp.einsum("tkjl,klm->tkjm", left_sym, prefix, precision=precise)
    left_full = jnp.einsum("kji,tkjm->tkim", prefix, partway, precision=precise)
    partway = jnp.einsum("kij,tkjl->tkil", suffix, right_sym, precision=precise)
    right_full = jnp.einsum("tkil,kml->tkim", partway, suffix, precision=precise)

    def partial_term(vector):
        halfway = jnp.einsum("tkij,kjl->tkil", left_full, vector, precision=precise)
        return jnp.einsum("tkil,tklm->kim", halfway, right_full, precision=precise)

    def finish(summed):
        return live_mask * summed

    started = live_mask * psi_guess[0]
    start_norm = jnp.sqrt(jnp.sum(started * started) / volume + epsilon)
    vector = started / start_norm

    def apply_whole(direction):
        return finish(lax.psum(partial_term(direction), "term"))

    def mean_dot(first_arr, second_arr):
        return jnp.sum(first_arr * second_arr) / volume

    image = apply_whole(vector)
    energy = mean_dot(vector, image)
    for step_index in range(ITERS):
        residual = image - energy * vector
        res_norm = jnp.sqrt(mean_dot(residual, residual) + epsilon)
        along = mean_dot(residual, image) / res_norm
        unit_dir = residual / res_norm
        image_unit = apply_whole(unit_dir)
        curve = mean_dot(unit_dir, image_unit)
        gap_half = 0.5 * (curve - energy)
        lowest = 0.5 * (curve + energy) - jnp.sqrt(gap_half * gap_half + along * along)
        coef_b = lowest - energy
        combined = jnp.sqrt(along * along + coef_b * coef_b)
        vector = (along * vector + coef_b * unit_dir) / combined
        image = (along * image + coef_b * image_unit) / combined
        energy = lowest
    vector_share = lax.dynamic_slice_in_dim(vector, offset, owned, 0)
    return (vector_share[None], jnp.reshape(energy, (1,)))


def solution(mesh):
    placed = (
        P("chain", None, None, None),
        P("chain", None, None, None),
        P("chain", "term", None, None, None),
        P("chain", "term", None, None, None),
        P("chain", None, None),
    )
    return jax.shard_map(
        local,
        mesh=mesh,
        in_specs=placed,
        out_specs=(P("chain", "term", None, None), P("chain")),
        check_vma=False,
    )
```

profile of v0, /device:TPU:2, one launch (start us, length us, event | category | flops | bytes accessed | tf_op | source)
XLA Modules:
  0.0 458.2 jit_solution(8209784709253944239)
XLA Ops:
  7.2 0.0 copy-start.11
  7.2 0.0 copy-start.12
  7.2 0.0 copy-start.7
  7.2 0.0 all-reduce.6.cloned.1.call-start
  7.2 5.4 %copy.8 = f32[1,8,8,128,128]{3,4,2,1,0:T(8,128)} copy(f32[1,8,8,128,128]{4,3,2,1,0:T(8,128)} %param.7) | data formatting | bytes 8388608 | tf_op args[2]
  12.7 1.9 collective-permute-start.1
  14.6 3.6 collective-permute-start.3
  18.3 0.2 copy.7
  18.5 0.1 fusion.73
  18.6 3.9 collective-permute-start.2
  22.5 1.9 collective-permute-start
  24.4 0.1 fusion.91
  24.5 0.8 multiply_reduce_fusion.12
  26.0 36.8 %collective-permute-done.1 = f32[8,8,128,128]{2,3,1,0:T(8,128)} collective-permute-done((f32[8,8,128,128]{2,3,1,0:T(8,128)}, f32[8,8,128,128]{2,3,1,0:T(8,128)}, u32[]{:S(2)}, u32[]{:S(2)}) %collective-permute-start.1) | collective-permute-done | bytes 4194336 | tf_op jit(solution)/shard_map/ppermute | solution.py:17
  62.8 6.5 %broadcast_select_fusion.1 = f32[8,8,128,128]{2,3,1,0:T(8,128)} fusion(f32[8,8,128,128]{2,3,1,0:T(8,128)} %collective-permute-done.1, pred[]{:T(512)S(6)} %eq.18, f32[1,8,8,128,128]{3,4,2,1,0:T(8,128)} %copy.8), kind=kLoop, calls=%fused_computation.38 | loop fusion | flops 1048576 | bytes 12582913 | tf_op jit(solution)/shard_map/jit(_where)/select_n | solution.py:53
  69.3 5.5 %copy.9 = f32[8,8,128,128]{3,2,1,0:T(8,128)} copy(f32[8,8,128,128]{2,3,1,0:T(8,128)} %broadcast_select_fusion.1) | data formatting | bytes 8388608 | tf_op jit(solution)/shard_map/jit(_where)/select_n | solution.py:53
  74.8 0.0 collective-permute-done.3
  74.8 6.7 %broadcast_select_fusion = f32[8,8,128,128]{3,2,1,0:T(8,128)} fusion(f32[8,8,128,128]{3,2,1,0:T(8,128)} %collective-permute-done.3, pred[]{:T(512)S(6)} %eq.20, f32[1,8,8,128,128]{4,3,2,1,0:T(8,128)} %param.8), kind=kLoop, calls=%fused_computation.37 | loop fusion | flops 1048576 | bytes 12582913 | tf_op jit(solution)/shard_map/jit(_where)/select_n | solution.py:54
  81.5 0.0 collective-permute-done
  81.5 0.0 copy-done.8
  81.5 4.2 fusion.33
  85.7 5.1 %fusion.28 = f32[8,8,128,128]{3,2,1,0:T(8,128)} fusion(f32[8,128,8,128]{3,1,2,0:T(8,128)S(1)} %fusion.33, f32[8,128,128]{2,1,0:T(8,128)S(1)} %collective-permute-done, f32[128,128]{1,0:T(8,128)S(1)} %fusion.90, pred[]{:T(512)S(6)} %eq.18), kind=kOutput, calls=%fused_computation.29 | convolution fusion | flops 1610743808 | bytes 8978433 | tf_op jit(solution)/shard_map/kji,tkjm->tkim/dot_general | solution.py:61
  90.8 5.3 %copy.10 = f32[8,8,128,128]{2,3,1,0:T(8,128)} copy(f32[8,8,128,128]{3,2,1,0:T(8,128)} %broadcast_select_fusion) | data formatting | bytes 8388608 | tf_op jit(solution)/shard_map/jit(_where)/select_n | solution.py:54
  96.1 9.0 %fusion.26 = f32[8,128,8,128]{1,3,2,0:T(8,128)S(1)} fusion(f32[8,8,128,128]{3,2,1,0:T(8,128)} %fusion.28, f32[1,8,128,128]{3,2,1,0:T(8,128)S(1)} %copy-done.7, f32[]{:T(128)S(6)} %sqrt.39, f32[8,128]{1,0:T(8,128)S(1)} %get-tuple-element.21, f32[8,128]{1,0:T(8,128)S(1)} %get-tuple-element.20), kind=kOutput, calls=%fused_computation.27 | convolution fusion | flops 1611005952 | bytes 8921092 | tf_op jit(solution)/shard_map/tkij,kjl->tkil/dot_general | solution.py:66
  105.2 0.0 collective-permute-done.2
  105.2 4.4 fusion.31
  109.6 4.3 fusion.14
  113.9 2.0 copy-done
  115.9 5.3 %fusion.35 = f32[8,128,128]{2,1,0:T(8,128)} fusion(f32[8,128,8,128]{3,1,2,0:T(8,128)S(1)} %fusion.14, f32[8,128,8,128]{1,3,2,0:T(8,128)S(1)} %fusion.26), kind=kOutput, calls=%fused_computation.45 | convolution fusion | flops 1610612736 | bytes 8912896 | tf_op jit(solution)/shard_map/tkil,tklm->kim/dot_general | solution.py:67
  121.1 0.0 all-reduce.6.cloned.1.call-update
  121.2 0.0 all-reduce.8.cloned.1.call-start
  121.2 52.0 %all-reduce.6.cloned.1.call-done = f32[8,128,128]{2,1,0:T(8,128)} async-done(((f32[8,128,128]{2,1,0:T(8,128)}), f32[8,128,128]{2,1,0:T(8,128)}) %all-reduce.6.cloned.1.call-update) | async-done | bytes 524304 | tf_op jit(solution)/shard_map/psum | solution.py:77
  173.3 1.9 multiply_reduce_fusion.11
  175.8 1.9 multiply_reduce_fusion.9
  178.3 0.0 copy-start.1
  178.3 8.9 %fusion.24 = f32[8,128,8,128]{1,3,2,0:T(8,128)S(1)} fusion(f32[8,8,128,128]{3,2,1,0:T(8,128)} %fusion.28, f32[]{:T(128)S(6)} %sqrt.40, f32[]{:T(128)S(6)} %div.131, f32[8,128,128]{2,1,0:T(8,128)} %all-reduce.6.cloned.1.call-done, f32[8,128]{1,0:T(8,128)S(1)} %get-tuple-element.21, f32[8,128]{1,0:T(8,128)S(1)} %get-tuple-element.20, ...), kind=kOutput, calls=%fused_computation.25 | convolution fusion | flops 1611530240 | bytes 9445388 | tf_op jit(solution)/shard_map/tkij,kjl->tkil/dot_general | solution.py:66
  187.3 4.8 %fusion.40 = f32[8,128,128]{2,1,0:T(8,128)} fusion(f32[8,128,8,128]{3,1,2,0:T(8,128)S(1)} %copy-done.1, f32[8,128,8,128]{1,3,2,0:T(8,128)S(1)} %fusion.24), kind=kOutput, calls=%fused_computation.46 | convolution fusion | flops 1610612736 | bytes 8912896 | tf_op jit(solution)/shard_map/tkil,tklm->kim/dot_general | solution.py:67
  192.0 0.0 all-reduce.8.cloned.1.call-update
  192.1 0.0 all-reduce.10.cloned.1.call-start
  192.1 48.8 %all-reduce.8.cloned.1.call-done = f32[8,128,128]{2,1,0:T(8,128)} async-done(((f32[8,128,128]{2,1,0:T(8,128)}), f32[8,128,128]{2,1,0:T(8,128)}) %all-reduce.8.cloned.1.call-update) | async-done | bytes 524304 | tf_op jit(solution)/shard_map/psum | solution.py:77
  240.9 0.0 copy-done.10
  240.9 1.9 multiply_reduce_fusion.8
  244.3 2.1 multiply_reduce_fusion.6
  247.1 8.8 %fusion.22 = f32[8,128,8,128]{1,3,2,0:T(8,128)S(1)} fusion(f32[8,8,128,128]{3,2,1,0:T(8,128)} %fusion.28, f32[]{:T(128)S(6)} %sqrt.43, f32[8,128,128]{2,1,0:T(8,128)S(1)} %get-tuple-element.17, f32[8,128,128]{2,1,0:T(8,128)S(1)} %get-tuple-element.16, f32[]{:T(128)S(6)} %sub.54), kind=kOutput, calls=%fused_computation.23 | convolution fusion | flops 1611005952 | bytes 9437192 | tf_op jit(solution)/shard_map/tkij,kjl->tkil/dot_general | solution.py:66
  255.9 4.8 %fusion.45 = f32[8,128,128]{2,1,0:T(8,128)} fusion(f32[8,128,8,128]{3,1,2,0:T(8,128)S(1)} %copy-done.2, f32[8,128,8,128]{1,3,2,0:T(8,128)S(1)} %fusion.22), kind=kOutput, calls=%fused_computation.47 | convolution fusion | flops 1610612736 | bytes 8912896 | tf_op jit(solution)/shard_map/tkil,tklm->kim/dot_general | solution.py:67
  260.8 0.0 all-reduce.10.cloned.1.call-update
  260.8 0.0 all-reduce.12.cloned.1.call-start
  260.8 48.8 %all-reduce.10.cloned.1.call-done = f32[8,128,128]{2,1,0:T(8,128)} async-done(((f32[8,128,128]{2,1,0:T(8,128)}), f32[8,128,128]{2,1,0:T(8,128)}) %all-reduce.10.cloned.1.call-update) | async-done | bytes 524304 | tf_op jit(solution)/shard_map/psum | solution.py:77
  309.7 1.9 multiply_reduce_fusion.5
  313.0 2.0 multiply_reduce_fusion.3
  315.6 8.9 %fusion.20 = f32[8,128,8,128]{1,3,2,0:T(8,128)S(1)} fusion(f32[8,8,128,128]{3,2,1,0:T(8,128)} %fusion.28, f32[]{:T(128)S(6)} %sqrt.46, f32[8,128,128]{2,1,0:T(8,128)S(1)} %get-tuple-element.14, f32[8,128,128]{2,1,0:T(8,128)S(1)} %get-tuple-element.13, f32[]{:T(128)S(6)} %sub.58), kind=kOutput, calls=%fused_computation.21 | convolution fusion | flops 1611005952 | bytes 9437192 | tf_op jit(solution)/shard_map/tkij,kjl->tkil/dot_general | solution.py:66
  324.5 4.8 %fusion.50 = f32[8,128,128]{2,1,0:T(8,128)} fusion(f32[8,128,8,128]{3,1,2,0:T(8,128)S(1)} %copy-done.3, f32[8,128,8,128]{1,3,2,0:T(8,128)S(1)} %fusion.20), kind=kOutput, calls=%fused_computation.48 | convolution fusion | flops 1610612736 | bytes 8912896 | tf_op jit(solution)/shard_map/tkil,tklm->kim/dot_general | solution.py:67
  329.3 0.0 all-reduce.12.cloned.1.call-update
  329.4 0.0 all-reduce.14.cloned.1.call-start
  329.4 48.8 %all-reduce.12.cloned.1.call-done = f32[8,128,128]{2,1,0:T(8,128)} async-done(((f32[8,128,128]{2,1,0:T(8,128)}), f32[8,128,128]{2,1,0:T(8,128)}) %all-reduce.12.cloned.1.call-update) | async-done | bytes 524304 | tf_op jit(solution)/shard_map/psum | solution.py:77
  378.3 1.9 multiply_reduce_fusion.2
  381.6 2.0 multiply_reduce_fusion.1
  384.3 0.1 broadcast_divide_fusion
  384.3 8.9 %fusion.18 = f32[8,128,8,128]{1,3,2,0:T(8,128)S(1)} fusion(f32[8,8,128,128]{3,2,1,0:T(8,128)} %fusion.28, f32[8,128,128]{2,1,0:T(8,128)S(1)} %broadcast_divide_fusion), kind=kOutput, calls=%fused_computation.19 | convolution fusion | flops 1610612736 | bytes 8912896 | tf_op jit(solution)/shard_map/tkij,kjl->tkil/dot_general | solution.py:66
  393.2 4.8 %fusion.55 = f32[8,128,128]{2,1,0:T(8,128)} fusion(f32[8,128,8,128]{3,1,2,0:T(8,128)S(1)} %copy-done.4, f32[8,128,8,128]{1,3,2,0:T(8,128)S(1)} %fusion.18), kind=kOutput, calls=%fused_computation.49 | convolution fusion | flops 1610612736 | bytes 8912896 | tf_op jit(solution)/shard_map/tkil,tklm->kim/dot_general | solution.py:67
  398.0 0.0 all-reduce.14.cloned.1.call-update
  398.7 48.2 %all-reduce.14.cloned.1.call-done = f32[8,128,128]{2,1,0:T(8,128)} async-done(((f32[8,128,128]{2,1,0:T(8,128)}), f32[8,128,128]{2,1,0:T(8,128)}) %all-reduce.14.cloned.1.call-update) | async-done | bytes 524304 | tf_op jit(solution)/shard_map/psum | solution.py:77
  446.9 1.9 fusion.61
  449.5 0.7 fusion.89
  (21 shorter events, 0.1 us)
Async XLA Ops:
  7.2 11.1 %copy-start.11 = (f32[1,8,128,128]{3,2,1,0:T(8,128)S(1)}, f32[1,8,128,128]{3,2,1,0:T(8,128)}, u32[]{:S(2)}) copy-start(f32[1,8,128,128]{3,2,1,0:T(8,128)} %param.6) | copy-start | bytes 1572868
  7.2 17.2 %copy-start.12 = (s32[1,2,8]{2,1,0:T(2,128)S(1)}, s32[1,2,8]{2,1,0:T(2,128)}, u32[]{:S(2)}) copy-start(s32[1,2,8]{2,1,0:T(2,128)} %param.9) | copy-start | bytes 196
  7.2 17.3 %copy-start.7 = (f32[1,8,128,128]{3,2,1,0:T(8,128)S(1)}, f32[1,8,128,128]{3,2,1,0:T(8,128)}, u32[]{:S(2)}) copy-start(f32[1,8,128,128]{3,2,1,0:T(8,128)} %param.5) | copy-start | bytes 1572868
  7.2 166.1 %all-reduce.6.cloned.1.call-start = ((), (), s32[]{:S(2)}) async-start(), calls=%async_computation | async-start | bytes 1048576 | tf_op jit(solution)/shard_map/psum | solution.py:77
  12.7 50.1 %collective-permute-start.1 = (f32[8,8,128,128]{2,3,1,0:T(8,128)}, f32[8,8,128,128]{2,3,1,0:T(8,128)}, u32[]{:S(2)}, u32[]{:S(2)}) collective-permute-start(f32[8,8,128,128]{2,3,1,0:T(8,128)} %bitcast.173), channel_id=1, source_target_pairs={{0,4},{4,8},{8,12},{12,16},{16,20},{20,24},{24,28},{28,32},{32,36}... | collective-permute-start | bytes 12582920 | tf_op jit(solution)/shard_map/ppermute | solution.py:17
  14.6 60.2 %collective-permute-start.3 = (f32[8,8,128,128]{3,2,1,0:T(8,128)}, f32[8,8,128,128]{3,2,1,0:T(8,128)}, u32[]{:S(2)}, u32[]{:S(2)}) collective-permute-start(f32[8,8,128,128]{3,2,1,0:T(8,128)} %bitcast.174), channel_id=1, source_target_pairs={{4,0},{8,4},{12,8},{16,12},{20,16},{24,20},{28,24},{32,28},{36,32}... | collective-permute-start | bytes 12582920 | tf_op jit(solution)/shard_map/ppermute | solution.py:17
  18.6 86.6 %collective-permute-start.2 = (f32[8,128,128]{2,1,0:T(8,128)S(1)}, f32[8,128,128]{2,1,0:T(8,128)S(1)}, u32[]{:S(2)}, u32[]{:S(2)}) collective-permute-start(f32[8,128,128]{2,1,0:T(8,128)S(1)} %fusion.73), channel_id=1, source_target_pairs={{4,0},{8,4},{12,8},{16,12},{20,16},{24,20},{28,24},{32,28},{36,32}... | collective-permute-start | bytes 1572872 | tf_op jit(solution)/shard_map/ppermute | solution.py:17
  22.5 59.0 %collective-permute-start = (f32[8,128,128]{2,1,0:T(8,128)S(1)}, f32[8,128,128]{2,1,0:T(8,128)S(1)}, u32[]{:S(2)}, u32[]{:S(2)}) collective-permute-start(f32[8,128,128]{2,1,0:T(8,128)S(1)} %fusion.73), channel_id=1, source_target_pairs={{0,4},{4,8},{8,12},{12,16},{16,20},{20,24},{24,28},{28,32},{32,36}... | collective-permute-start | bytes 1572872 | tf_op jit(solution)/shard_map/ppermute | solution.py:17
  74.8 6.7 %copy-start.6 = (f32[8,8,128,128]{2,3,1,0:T(8,128)S(1)}, f32[8,8,128,128]{2,3,1,0:T(8,128)}, u32[]{:S(2)}) copy-start(f32[8,8,128,128]{2,3,1,0:T(8,128)} %broadcast_select_fusion.1) | copy-start | bytes 12582916
  74.8 6.7 %copy-start.8 = (f32[8,8,128,128]{3,2,1,0:T(8,128)S(1)}, f32[8,8,128,128]{3,2,1,0:T(8,128)}, u32[]{:S(2)}) copy-start(f32[8,8,128,128]{3,2,1,0:T(8,128)} %copy.9) | copy-start | bytes 12582916
  96.1 9.1 %copy-start.5 = (f32[8,8,128,128]{3,2,1,0:T(8,128)S(1)}, f32[8,8,128,128]{3,2,1,0:T(8,128)}, u32[]{:S(2)}) copy-start(f32[8,8,128,128]{3,2,1,0:T(8,128)} %broadcast_select_fusion) | copy-start | bytes 12582916
  96.1 9.1 %copy-start.9 = (f32[8,8,128,128]{2,3,1,0:T(8,128)S(1)}, f32[8,8,128,128]{2,3,1,0:T(8,128)}, u32[]{:S(2)}) copy-start(f32[8,8,128,128]{2,3,1,0:T(8,128)} %copy.10) | copy-start | bytes 12582916
  113.9 2.0 copy-start
  121.2 119.8 %all-reduce.8.cloned.1.call-start = ((), (), s32[]{:S(2)}) async-start(), calls=%async_computation.1 | async-start | bytes 1048576 | tf_op jit(solution)/shard_map/psum | solution.py:77
  178.3 8.9 %copy-start.1 = (f32[8,128,8,128]{3,1,2,0:T(8,128)S(1)}, f32[8,128,8,128]{3,1,2,0:T(8,128)}, u32[]{:S(2)}) copy-start(f32[8,128,8,128]{3,1,2,0:T(8,128)} %copy-done) | copy-start | bytes 12582916
  187.3 53.7 %copy-start.10 = (f32[8,128,128]{2,1,0:T(8,128)S(1)}, f32[8,128,128]{2,1,0:T(8,128)}, u32[]{:S(2)}) copy-start(f32[8,128,128]{2,1,0:T(8,128)} %all-reduce.6.cloned.1.call-done) | copy-start | bytes 1572868
  192.1 117.6 %all-reduce.10.cloned.1.call-start = ((), (), s32[]{:S(2)}) async-start(), calls=%async_computation.2 | async-start | bytes 1048576 | tf_op jit(solution)/shard_map/psum | solution.py:77
  247.1 8.8 %copy-start.2 = (f32[8,128,8,128]{3,1,2,0:T(8,128)S(1)}, f32[8,128,8,128]{3,1,2,0:T(8,128)}, u32[]{:S(2)}) copy-start(f32[8,128,8,128]{3,1,2,0:T(8,128)} %copy-done) | copy-start | bytes 12582916
  260.8 117.5 %all-reduce.12.cloned.1.call-start = ((), (), s32[]{:S(2)}) async-start(), calls=%async_computation.3 | async-start | bytes 1048576 | tf_op jit(solution)/shard_map/psum | solution.py:77
  315.6 8.9 %copy-start.3 = (f32[8,128,8,128]{3,1,2,0:T(8,128)S(1)}, f32[8,128,8,128]{3,1,2,0:T(8,128)}, u32[]{:S(2)}) copy-start(f32[8,128,8,128]{3,1,2,0:T(8,128)} %copy-done) | copy-start | bytes 12582916
  329.4 117.6 %all-reduce.14.cloned.1.call-start = ((), (), s32[]{:S(2)}) async-start(), calls=%async_computation.4 | async-start | bytes 1048576 | tf_op jit(solution)/shard_map/psum | solution.py:77
  384.3 8.9 %copy-start.4 = (f32[8,128,8,128]{3,1,2,0:T(8,128)S(1)}, f32[8,128,8,128]{3,1,2,0:T(8,128)}, u32[]{:S(2)}) copy-start(f32[8,128,8,128]{3,1,2,0:T(8,128)} %copy-done) | copy-start | bytes 12582916
Sparse Core Ops, SparseCore 0:
  121.3 51.9 all-reduce.5
  192.2 48.7 all-reduce.7
  260.9 48.7 all-reduce.9
  329.5 48.7 all-reduce.11
  398.2 48.7 all-reduce.13
where the time goes:
time: 461 us; the launch traced here: 458 us
  waiting for transfers between devices  284 us (62%)
  matrix products  86.9 us (19%)
  other arithmetic  32.2 us (7%)
  between operations  25.4 us (6%)
  local copies, waits for them, and re-layouts  18.5 us (4%)
  starting transfers between devices  11.6 us (3%)
    psum x5, waiting for transfers between devices, apply_whole(): return finish(lax.psum(partial_term(direction), 'term'))  247 us
    dot_general x5, matrix products, partial_term(): halfway = jnp.einsum('tkij,kjl->tkil', left_full, vector, precision=precise)  44.5 us
    ppermute x4, waiting for transfers between devices, from_behind(): lax.ppermute(value, axis, [(source, source + steps) for source in range(l...  36.8 us
    dot_general x5, matrix products, partial_term(): return jnp.einsum('tkil,tklm->kim', halfway, right_full, precision=precise)  24.4 us
    reduce_sum x9, other arithmetic, mean_dot(): return jnp.sum(first_arr * second_arr) / volume  17.2 us
    ppermute x4, starting transfers between devices, from_behind(): lax.ppermute(value, axis, [(source, source + steps) for source in range(l...  11.4 us
  transfers between devices with their start and end apart: 9, of which 6 were waited for; matrix products, arithmetic and copies ran while one was open for 9% of the time, Pallas kernels for 0%

commit v1 on v0

--- a/solution.py
+++ b/solution.py
@@ -74,7 +74,7 @@
     vector = started / start_norm
 
     def apply_whole(direction):
-        return finish(lax.psum(partial_term(direction), "term"))
+        return finish(jnp.sum(lax.all_gather(partial_term(direction), "term"), axis=0))
 
     def mean_dot(first_arr, second_arr):
         return jnp.sum(first_arr * second_arr) / volume

time: 461 us -> 385 us (0.84)
  waiting for transfers between devices: 284 us -> 208 us
    psum x5 -> x0, waiting for transfers between devices: 247 us -> none  [apply_whole(): return finish(lax.psum(partial_term(direction), 'term'))]
    all_gather x0 -> x5, waiting for transfers between devices: none -> 171 us  [apply_whole(): lax.all_gather(partial_term(direction), 'term')]
    reduce_sum x9, other arithmetic: 17.2 us -> 7.84 us  [mean_dot(): return jnp.sum(first_arr * second_arr) / volume]
    reduce_sum x0 -> x5, other arithmetic: none -> 8.8 us  [apply_whole(): jnp.sum(lax.all_gather(partial_term(direction), 'term'), axis=0)]
  transfers between devices with their start and end apart: 9 -> 9, of which waited for: 6 -> 6; matrix products, arithmetic and copies ran while one was open for 9% -> 11% of each run, Pallas kernels for 0% -> 0%
where the time goes in v1:
time: 385 us; the launch traced here: 381 us
  waiting for transfers between devices  208 us (54%)
  matrix products  86.7 us (23%)
  other arithmetic  31.6 us (8%)
  between operations  25.4 us (7%)
  local copies, waits for them, and re-layouts  18.5 us (5%)
  starting transfers between devices  11.6 us (3%)
    all_gather x5, waiting for transfers between devices, apply_whole(): lax.all_gather(partial_term(direction), 'term')  171 us
    dot_general x5, matrix products, partial_term(): halfway = jnp.einsum('tkij,kjl->tkil', left_full, vector, precision=precise)  44.4 us
    ppermute x4, waiting for transfers between devices, from_behind(): lax.ppermute(value, axis, [(source, source + steps) for source in range(l...  36.8 us
    dot_general x5, matrix products, partial_term(): return jnp.einsum('tkil,tklm->kim', halfway, right_full, precision=precise)  24.3 us
    ppermute x4, starting transfers between devices, from_behind(): lax.ppermute(value, axis, [(source, source + steps) for source in range(l...  11.4 us
    reduce_sum x5, other arithmetic, apply_whole(): jnp.sum(lax.all_gather(partial_term(direction), 'term'), axis=0)  8.8 us
    reduce_sum x9, other arithmetic, mean_dot(): return jnp.sum(first_arr * second_arr) / volume  7.84 us
  transfers between devices with their start and end apart: 9, of which 6 were waited for; matrix products, arithmetic and copies ran while one was open for 11% of the time, Pallas kernels for 0%

profile of v1, /device:TPU:2, one launch (start us, length us, event | category | flops | bytes accessed | tf_op | source)
XLA Modules:
  0.0 381.5 jit_solution(1138106757067383491)
XLA Ops:
  7.2 0.0 copy-start.10
  7.2 0.0 all-gather.11.cloned.1.call-start
  7.2 5.4 %copy.17 = f32[1,8,8,128,128]{3,4,2,1,0:T(8,128)} copy(f32[1,8,8,128,128]{4,3,2,1,0:T(8,128)} %param.7) | data formatting | bytes 8388608 | tf_op args[2]
  12.7 1.9 collective-permute-start.1
  14.6 3.6 collective-permute-start.3
  18.3 0.2 copy.16
  18.5 0.1 fusion.73
  18.6 3.9 %collective-permute-start.2 = (f32[8,128,128]{2,1,0:T(8,128)S(1)}, f32[8,128,128]{2,1,0:T(8,128)S(1)}, u32[]{:S(2)}, u32[]{:S(2)}) collective-permute-start(f32[8,128,128]{2,1,0:T(8,128)S(1)} %fusion.73), channel_id=1, source_target_pairs={{4,0},{8,4},{12,8},{16,12},{20,16},{24,20},{28,24},{32,28},{36,32}... | collective-permute-start | bytes 1572872 | tf_op jit(solution)/shard_map/ppermute | solution.py:17
  22.5 1.9 collective-permute-start
  24.4 0.1 fusion.91
  24.5 0.8 multiply_reduce_fusion.12
  26.0 36.8 %collective-permute-done.1 = f32[8,8,128,128]{2,3,1,0:T(8,128)} collective-permute-done((f32[8,8,128,128]{2,3,1,0:T(8,128)}, f32[8,8,128,128]{2,3,1,0:T(8,128)}, u32[]{:S(2)}, u32[]{:S(2)}) %collective-permute-start.1) | collective-permute-done | bytes 4194336 | tf_op jit(solution)/shard_map/ppermute | solution.py:17
  62.8 6.5 %broadcast_select_fusion.1 = f32[8,8,128,128]{2,3,1,0:T(8,128)} fusion(f32[8,8,128,128]{2,3,1,0:T(8,128)} %collective-permute-done.1, pred[]{:T(512)S(6)} %eq.18, f32[1,8,8,128,128]{3,4,2,1,0:T(8,128)} %copy.17), kind=kLoop, calls=%fused_computation.38 | loop fusion | flops 1048576 | bytes 12582913 | tf_op jit(solution)/shard_map/jit(_where)/select_n | solution.py:53
  69.3 5.5 %copy.18 = f32[8,8,128,128]{3,2,1,0:T(8,128)} copy(f32[8,8,128,128]{2,3,1,0:T(8,128)} %broadcast_select_fusion.1) | data formatting | bytes 8388608 | tf_op jit(solution)/shard_map/jit(_where)/select_n | solution.py:53
  74.8 0.0 collective-permute-done.3
  74.8 6.7 %broadcast_select_fusion = f32[8,8,128,128]{3,2,1,0:T(8,128)} fusion(f32[8,8,128,128]{3,2,1,0:T(8,128)} %collective-permute-done.3, pred[]{:T(512)S(6)} %eq.20, f32[1,8,8,128,128]{4,3,2,1,0:T(8,128)} %param.8), kind=kLoop, calls=%fused_computation.37 | loop fusion | flops 1048576 | bytes 12582913 | tf_op jit(solution)/shard_map/jit(_where)/select_n | solution.py:54
  81.5 0.0 collective-permute-done
  81.5 4.2 %fusion.33 = f32[8,128,8,128]{3,1,2,0:T(8,128)S(1)} fusion(f32[8,128,128]{2,1,0:T(8,128)S(1)} %collective-permute-done, f32[128,128]{1,0:T(8,128)S(1)} %fusion.90, pred[]{:T(512)S(6)} %eq.18, f32[8,8,128,128]{3,2,1,0:T(8,128)S(1)} %copy-done.8, f32[8,8,128,128]{2,3,1,0:T(8,128)S(1)} %copy-done.6), kind=kOutput, calls=%fused_computation.35 | convolution fusion | flops 1612840960 | bytes 13172737 | tf_op jit(solution)/shard_map/tkjl,klm->tkjm/dot_general | solution.py:60
  85.7 5.1 %fusion.28 = f32[8,8,128,128]{3,2,1,0:T(8,128)} fusion(f32[8,128,8,128]{3,1,2,0:T(8,128)S(1)} %fusion.33, f32[8,128,128]{2,1,0:T(8,128)S(1)} %collective-permute-done, f32[128,128]{1,0:T(8,128)S(1)} %fusion.90, pred[]{:T(512)S(6)} %eq.18), kind=kOutput, calls=%fused_computation.29 | convolution fusion | flops 1610743808 | bytes 8978433 | tf_op jit(solution)/shard_map/kji,tkjm->tkim/dot_general | solution.py:61
  90.8 5.3 %copy.19 = f32[8,8,128,128]{2,3,1,0:T(8,128)} copy(f32[8,8,128,128]{3,2,1,0:T(8,128)} %broadcast_select_fusion) | data formatting | bytes 8388608 | tf_op jit(solution)/shard_map/jit(_where)/select_n | solution.py:54
  96.1 9.0 %fusion.26 = f32[8,128,8,128]{1,3,2,0:T(8,128)S(1)} fusion(f32[8,8,128,128]{3,2,1,0:T(8,128)} %fusion.28, f32[1,8,128,128]{3,2,1,0:T(8,128)S(1)} %copy-done.7, f32[]{:T(128)S(6)} %sqrt.39, f32[8,128]{1,0:T(8,128)S(1)} %get-tuple-element.21, f32[8,128]{1,0:T(8,128)S(1)} %get-tuple-element.20), kind=kOutput, calls=%fused_computation.27 | convolution fusion | flops 1611005952 | bytes 8921092 | tf_op jit(solution)/shard_map/tkij,kjl->tkil/dot_general | solution.py:66
  105.2 0.0 collective-permute-done.2
  105.2 4.4 %fusion.31 = f32[8,8,128,128]{2,3,1,0:T(8,128)S(1)} fusion(f32[8,128,128]{2,1,0:T(8,128)S(1)} %collective-permute-done.2, f32[128,128]{1,0:T(8,128)S(1)} %fusion.90, pred[]{:T(512)S(6)} %eq.20, f32[8,8,128,128]{3,2,1,0:T(8,128)S(1)} %copy-done.5, f32[8,8,128,128]{2,3,1,0:T(8,128)S(1)} %copy-done.9), kind=kOutput, calls=%fused_computation.33 | convolution fusion | flops 1612840960 | bytes 13172737 | tf_op jit(solution)/shard_map/kij,tkjl->tkil/dot_general | solution.py:62
  109.6 4.3 %fusion.14 = f32[8,128,8,128]{3,1,2,0:T(8,128)S(1)} fusion(f32[8,8,128,128]{2,3,1,0:T(8,128)S(1)} %fusion.31, f32[8,128,128]{2,1,0:T(8,128)S(1)} %collective-permute-done.2, f32[128,128]{1,0:T(8,128)S(1)} %fusion.90, pred[]{:T(512)S(6)} %eq.20), kind=kOutput, calls=%fused_computation.14 | convolution fusion | flops 1610743808 | bytes 8978433 | tf_op jit(solution)/shard_map/tkil,kml->tkim/dot_general | solution.py:63
  113.9 2.0 copy-done
  115.9 5.2 %fusion.35 = f32[8,128,128]{2,1,0:T(8,128)} fusion(f32[8,128,8,128]{3,1,2,0:T(8,128)S(1)} %fusion.14, f32[8,128,8,128]{1,3,2,0:T(8,128)S(1)} %fusion.26), kind=kOutput, calls=%fused_computation.45 | convolution fusion | flops 1610612736 | bytes 8912896 | tf_op jit(solution)/shard_map/tkil,tklm->kim/dot_general | solution.py:67
  121.1 0.0 all-gather.11.cloned.1.call-update
  121.1 0.0 all-gather.13.cloned.1.call-start
  121.2 37.3 %all-gather.11.cloned.1.call-done = f32[32,128,128]{2,1,0:T(8,128)} async-done(((f32[8,128,128]{2,1,0:T(8,128)}), f32[32,128,128]{2,1,0:T(8,128)}) %all-gather.11.cloned.1.call-update) | async-done | bytes 2097168 | tf_op jit(solution)/shard_map/all_gather | solution.py:77
  158.5 1.8 reduce_sum.172
  160.3 0.8 multiply_reduce_fusion.11
  161.7 0.8 multiply_reduce_fusion.9
  163.2 8.8 %fusion.24 = f32[8,128,8,128]{1,3,2,0:T(8,128)S(1)} fusion(f32[8,8,128,128]{3,2,1,0:T(8,128)} %fusion.28, f32[]{:T(128)S(6)} %sqrt.40, f32[]{:T(128)S(6)} %div.131, f32[8,128,128]{2,1,0:T(8,128)S(1)} %reduce_sum.172, f32[8,128]{1,0:T(8,128)S(1)} %get-tuple-element.21, f32[8,128]{1,0:T(8,128)S(1)} %get-tuple-element.20, ...), kind=kOutput, calls=%fused_computation.25 | convolution fusion | flops 1611530240 | bytes 9445388 | tf_op jit(solution)/shard_map/tkij,kjl->tkil/dot_general | solution.py:66
  172.1 4.8 %fusion.40 = f32[8,128,128]{2,1,0:T(8,128)} fusion(f32[8,128,8,128]{3,1,2,0:T(8,128)S(1)} %copy-done.1, f32[8,128,8,128]{1,3,2,0:T(8,128)S(1)} %fusion.24), kind=kOutput, calls=%fused_computation.46 | convolution fusion | flops 1610612736 | bytes 8912896 | tf_op jit(solution)/shard_map/tkil,tklm->kim/dot_general | solution.py:67
  176.9 0.0 all-gather.13.cloned.1.call-update
  176.9 0.0 all-gather.15.cloned.1.call-start
  176.9 33.6 %all-gather.13.cloned.1.call-done = f32[32,128,128]{2,1,0:T(8,128)} async-done(((f32[8,128,128]{2,1,0:T(8,128)}), f32[32,128,128]{2,1,0:T(8,128)}) %all-gather.13.cloned.1.call-update) | async-done | bytes 2097168 | tf_op jit(solution)/shard_map/all_gather | solution.py:77
  210.5 1.8 reduce_sum.176
  212.3 0.9 multiply_reduce_fusion.8
  214.6 1.0 multiply_reduce_fusion.6
  216.3 8.8 %fusion.22 = f32[8,128,8,128]{1,3,2,0:T(8,128)S(1)} fusion(f32[8,8,128,128]{3,2,1,0:T(8,128)} %fusion.28, f32[]{:T(128)S(6)} %sqrt.43, f32[8,128,128]{2,1,0:T(8,128)S(1)} %get-tuple-element.17, f32[8,128,128]{2,1,0:T(8,128)S(1)} %get-tuple-element.16, f32[]{:T(128)S(6)} %sub.54), kind=kOutput, calls=%fused_computation.23 | convolution fusion | flops 1611005952 | bytes 9437192 | tf_op jit(solution)/shard_map/tkij,kjl->tkil/dot_general | solution.py:66
  225.1 4.8 %fusion.45 = f32[8,128,128]{2,1,0:T(8,128)} fusion(f32[8,128,8,128]{3,1,2,0:T(8,128)S(1)} %copy-done.2, f32[8,128,8,128]{1,3,2,0:T(8,128)S(1)} %fusion.22), kind=kOutput, calls=%fused_computation.47 | convolution fusion | flops 1610612736 | bytes 8912896 | tf_op jit(solution)/shard_map/tkil,tklm->kim/dot_general | solution.py:67
  229.9 0.0 all-gather.15.cloned.1.call-update
  230.0 0.0 all-gather.17.cloned.1.call-start
  230.0 33.6 %all-gather.15.cloned.1.call-done = f32[32,128,128]{2,1,0:T(8,128)} async-done(((f32[8,128,128]{2,1,0:T(8,128)}), f32[32,128,128]{2,1,0:T(8,128)}) %all-gather.15.cloned.1.call-update) | async-done | bytes 2097168 | tf_op jit(solution)/shard_map/all_gather | solution.py:77
  263.6 1.8 reduce_sum.180
  265.3 0.8 multiply_reduce_fusion.5
  267.6 0.9 multiply_reduce_fusion.3
  269.2 8.9 %fusion.20 = f32[8,128,8,128]{1,3,2,0:T(8,128)S(1)} fusion(f32[8,8,128,128]{3,2,1,0:T(8,128)} %fusion.28, f32[]{:T(128)S(6)} %sqrt.46, f32[8,128,128]{2,1,0:T(8,128)S(1)} %get-tuple-element.14, f32[8,128,128]{2,1,0:T(8,128)S(1)} %get-tuple-element.13, f32[]{:T(128)S(6)} %sub.58), kind=kOutput, calls=%fused_computation.21 | convolution fusion | flops 1611005952 | bytes 9437192 | tf_op jit(solution)/shard_map/tkij,kjl->tkil/dot_general | solution.py:66
  278.1 4.8 %fusion.50 = f32[8,128,128]{2,1,0:T(8,128)} fusion(f32[8,128,8,128]{3,1,2,0:T(8,128)S(1)} %copy-done.3, f32[8,128,8,128]{1,3,2,0:T(8,128)S(1)} %fusion.20), kind=kOutput, calls=%fused_computation.48 | convolution fusion | flops 1610612736 | bytes 8912896 | tf_op jit(solution)/shard_map/tkil,tklm->kim/dot_general | solution.py:67
  282.9 0.0 all-gather.17.cloned.1.call-update
  282.9 0.0 all-gather.19.cloned.1.call-start
  282.9 33.5 %all-gather.17.cloned.1.call-done = f32[32,128,128]{2,1,0:T(8,128)} async-done(((f32[8,128,128]{2,1,0:T(8,128)}), f32[32,128,128]{2,1,0:T(8,128)}) %all-gather.17.cloned.1.call-update) | async-done | bytes 2097168 | tf_op jit(solution)/shard_map/all_gather | solution.py:77
  316.5 1.8 reduce_sum.184
  318.3 0.8 multiply_reduce_fusion.2
  320.5 0.9 multiply_reduce_fusion.1
  322.2 0.1 broadcast_divide_fusion
  322.2 8.9 %fusion.18 = f32[8,128,8,128]{1,3,2,0:T(8,128)S(1)} fusion(f32[8,8,128,128]{3,2,1,0:T(8,128)} %fusion.28, f32[8,128,128]{2,1,0:T(8,128)S(1)} %broadcast_divide_fusion), kind=kOutput, calls=%fused_computation.19 | convolution fusion | flops 1610612736 | bytes 8912896 | tf_op jit(solution)/shard_map/tkij,kjl->tkil/dot_general | solution.py:66
  331.1 4.8 %fusion.55 = f32[8,128,128]{2,1,0:T(8,128)} fusion(f32[8,128,8,128]{3,1,2,0:T(8,128)S(1)} %copy-done.4, f32[8,128,8,128]{1,3,2,0:T(8,128)S(1)} %fusion.18), kind=kOutput, calls=%fused_computation.49 | convolution fusion | flops 1610612736 | bytes 8912896 | tf_op jit(solution)/shard_map/tkil,tklm->kim/dot_general | solution.py:67
  335.9 0.0 all-gather.19.cloned.1.call-update
  336.6 32.9 %all-gather.19.cloned.1.call-done = f32[32,128,128]{2,1,0:T(8,128)} async-done(((f32[8,128,128]{2,1,0:T(8,128)}), f32[32,128,128]{2,1,0:T(8,128)}) %all-gather.19.cloned.1.call-update) | async-done | bytes 2097168 | tf_op jit(solution)/shard_map/all_gather | solution.py:77
  369.5 1.8 reduce_sum.188
  371.3 0.8 fusion.61
  372.9 0.7 fusion.89
  (24 shorter events, 0.1 us)
Async XLA Ops:
  7.2 11.1 %copy-start.10 = (f32[1,8,128,128]{3,2,1,0:T(8,128)S(1)}, f32[1,8,128,128]{3,2,1,0:T(8,128)}, u32[]{:S(2)}) copy-start(f32[1,8,128,128]{3,2,1,0:T(8,128)} %param.6) | copy-start | bytes 1572868
  7.2 17.2 %copy-start.11 = (s32[1,2,8]{2,1,0:T(2,128)S(1)}, s32[1,2,8]{2,1,0:T(2,128)}, u32[]{:S(2)}) copy-start(s32[1,2,8]{2,1,0:T(2,128)} %param.9) | copy-start | bytes 196
  7.2 17.3 %copy-start.7 = (f32[1,8,128,128]{3,2,1,0:T(8,128)S(1)}, f32[1,8,128,128]{3,2,1,0:T(8,128)}, u32[]{:S(2)}) copy-start(f32[1,8,128,128]{3,2,1,0:T(8,128)} %param.5) | copy-start | bytes 1572868
  7.2 151.3 %all-gather.11.cloned.1.call-start = ((), (), s32[]{:S(2)}) async-start(), calls=%async_computation | async-start | bytes 2621440 | tf_op jit(solution)/shard_map/all_gather | solution.py:77
  12.7 50.1 %collective-permute-start.1 = (f32[8,8,128,128]{2,3,1,0:T(8,128)}, f32[8,8,128,128]{2,3,1,0:T(8,128)}, u32[]{:S(2)}, u32[]{:S(2)}) collective-permute-start(f32[8,8,128,128]{2,3,1,0:T(8,128)} %bitcast.178), channel_id=1, source_target_pairs={{0,4},{4,8},{8,12},{12,16},{16,20},{20,24},{24,28},{28,32},{32,36}... | collective-permute-start | bytes 12582920 | tf_op jit(solution)/shard_map/ppermute | solution.py:17
  14.6 60.2 %collective-permute-start.3 = (f32[8,8,128,128]{3,2,1,0:T(8,128)}, f32[8,8,128,128]{3,2,1,0:T(8,128)}, u32[]{:S(2)}, u32[]{:S(2)}) collective-permute-start(f32[8,8,128,128]{3,2,1,0:T(8,128)} %bitcast.179), channel_id=1, source_target_pairs={{4,0},{8,4},{12,8},{16,12},{20,16},{24,20},{28,24},{32,28},{36,32}... | collective-permute-start | bytes 12582920 | tf_op jit(solution)/shard_map/ppermute | solution.py:17
  18.6 86.6 %collective-permute-start.2 = (f32[8,128,128]{2,1,0:T(8,128)S(1)}, f32[8,128,128]{2,1,0:T(8,128)S(1)}, u32[]{:S(2)}, u32[]{:S(2)}) collective-permute-start(f32[8,128,128]{2,1,0:T(8,128)S(1)} %fusion.73), channel_id=1, source_target_pairs={{4,0},{8,4},{12,8},{16,12},{20,16},{24,20},{28,24},{32,28},{36,32}... | collective-permute-start | bytes 1572872 | tf_op jit(solution)/shard_map/ppermute | solution.py:17
  22.5 59.0 %collective-permute-start = (f32[8,128,128]{2,1,0:T(8,128)S(1)}, f32[8,128,128]{2,1,0:T(8,128)S(1)}, u32[]{:S(2)}, u32[]{:S(2)}) collective-permute-start(f32[8,128,128]{2,1,0:T(8,128)S(1)} %fusion.73), channel_id=1, source_target_pairs={{0,4},{4,8},{8,12},{12,16},{16,20},{20,24},{24,28},{28,32},{32,36}... | collective-permute-start | bytes 1572872 | tf_op jit(solution)/shard_map/ppermute | solution.py:17
  74.8 6.7 %copy-start.6 = (f32[8,8,128,128]{2,3,1,0:T(8,128)S(1)}, f32[8,8,128,128]{2,3,1,0:T(8,128)}, u32[]{:S(2)}) copy-start(f32[8,8,128,128]{2,3,1,0:T(8,128)} %broadcast_select_fusion.1) | copy-start | bytes 12582916
  74.8 6.7 %copy-start.8 = (f32[8,8,128,128]{3,2,1,0:T(8,128)S(1)}, f32[8,8,128,128]{3,2,1,0:T(8,128)}, u32[]{:S(2)}) copy-start(f32[8,8,128,128]{3,2,1,0:T(8,128)} %copy.18) | copy-start | bytes 12582916
  96.1 9.1 %copy-start.5 = (f32[8,8,128,128]{3,2,1,0:T(8,128)S(1)}, f32[8,8,128,128]{3,2,1,0:T(8,128)}, u32[]{:S(2)}) copy-start(f32[8,8,128,128]{3,2,1,0:T(8,128)} %broadcast_select_fusion) | copy-start | bytes 12582916
  96.1 9.1 %copy-start.9 = (f32[8,8,128,128]{2,3,1,0:T(8,128)S(1)}, f32[8,8,128,128]{2,3,1,0:T(8,128)}, u32[]{:S(2)}) copy-start(f32[8,8,128,128]{2,3,1,0:T(8,128)} %copy.19) | copy-start | bytes 12582916
  113.9 2.0 copy-start
  121.1 89.4 %all-gather.13.cloned.1.call-start = ((), (), s32[]{:S(2)}) async-start(), calls=%async_computation.1 | async-start | bytes 2621440 | tf_op jit(solution)/shard_map/all_gather | solution.py:77
  163.2 8.8 %copy-start.1 = (f32[8,128,8,128]{3,1,2,0:T(8,128)S(1)}, f32[8,128,8,128]{3,1,2,0:T(8,128)}, u32[]{:S(2)}) copy-start(f32[8,128,8,128]{3,1,2,0:T(8,128)} %copy-done) | copy-start | bytes 12582916
  176.9 86.7 %all-gather.15.cloned.1.call-start = ((), (), s32[]{:S(2)}) async-start(), calls=%async_computation.2 | async-start | bytes 2621440 | tf_op jit(solution)/shard_map/all_gather | solution.py:77
  216.3 8.8 %copy-start.2 = (f32[8,128,8,128]{3,1,2,0:T(8,128)S(1)}, f32[8,128,8,128]{3,1,2,0:T(8,128)}, u32[]{:S(2)}) copy-start(f32[8,128,8,128]{3,1,2,0:T(8,128)} %copy-done) | copy-start | bytes 12582916
  230.0 86.5 %all-gather.17.cloned.1.call-start = ((), (), s32[]{:S(2)}) async-start(), calls=%async_computation.3 | async-start | bytes 2621440 | tf_op jit(solution)/shard_map/all_gather | solution.py:77
  269.2 8.9 %copy-start.3 = (f32[8,128,8,128]{3,1,2,0:T(8,128)S(1)}, f32[8,128,8,128]{3,1,2,0:T(8,128)}, u32[]{:S(2)}) copy-start(f32[8,128,8,128]{3,1,2,0:T(8,128)} %copy-done) | copy-start | bytes 12582916
  282.9 86.6 %all-gather.19.cloned.1.call-start = ((), (), s32[]{:S(2)}) async-start(), calls=%async_computation.4 | async-start | bytes 2621440 | tf_op jit(solution)/shard_map/all_gather | solution.py:77
  322.2 8.9 %copy-start.4 = (f32[8,128,8,128]{3,1,2,0:T(8,128)S(1)}, f32[8,128,8,128]{3,1,2,0:T(8,128)}, u32[]{:S(2)}) copy-start(f32[8,128,8,128]{3,1,2,0:T(8,128)} %copy-done) | copy-start | bytes 12582916
Sparse Core Ops, SparseCore 0:
  121.2 37.2 all-gather.10
  177.0 33.4 all-gather.12
  230.1 33.4 all-gather.14
  283.0 33.4 all-gather.16
  336.1 33.4 all-gather.18
